TPU v7x, 256 devices: a whole 4x4x8 slice. The times are simulated.
256 devices in a mesh: cuts: 8 (over x, y_lo), layer: 32 (over z, y_hi, core).
Axes of the slice: x: 4, y: 4 (y_hi: 2, y_lo: 2; y = y_hi * 2 + y_lo), z: 8, core: 2. Of those that a mesh axis runs over, the one named last changes fastest.
Arguments:
- vectors: float32 [8, 64, 64, 1024], P('cuts', None, 'layer'), may hold values from -40 to 40
- diag_blocks: bfloat16 [64, 1024, 1024], P('layer'), may hold values from -1 to 1, as said below
- couplings: bfloat16 [64, 1024, 1024], P('layer'), may hold values from -0.09375 to 0.09375
- bounds: int32 [8, 2], P('cuts'), may hold values from -128 to 160, as said below
Outputs:
- filtered: float32 [8, 64, 64, 1024], P('cuts', None, 'layer')
Inputs may be any that keep to these rules, and one draw needn't show every extreme that they name: `bounds`: column 0 holds each slice's lower end, which is -128 at slice 0 and to at most -81; column 1 holds its upper end, from 128 to 160. `diag_blocks`: each block is symmetric.
All inputs are finite; a program needn't handle non-finite values.
Results may differ from a plain program's by a relative error of at most 0.012.
Values may be sent and summed in bfloat16 or wider, within the bound.
A program may use at most 64 MiB of HBM per device.

v0:
```python
import jax
import jax.numpy as jnp
from jax import lax
from jax.sharding import PartitionSpec as P

EDGE = 16
DEG = 4


def shifted(block, axis, distance):
    devices = range(lax.axis_size(axis))
    route = [(i - distance, i) for i in devices if i - distance in devices]
    return lax.ppermute(block, axis, route)


def extended(block, sides, width):
    for axis, dim in sides:
        count = lax.axis_size(axis)
        forward = [(i, i + 1) for i in range(count - 1)]
        backward = [(target, source) for source, target in forward]
        low = lax.ppermute(
            lax.slice_in_dim(block, block.shape[dim] - width, None, axis=dim), axis, forward
        )
        high = lax.ppermute(lax.slice_in_dim(block, 0, width, axis=dim), axis, backward)
        block = jnp.concatenate([low, block, high], axis=dim)
    return block


def inner_products(first, second):
    return jnp.einsum("kn,jn->kj", first, second, precision=lax.Precision.HIGHEST)


def left_solve(factor, right_side):
    return lax.linalg.triangular_solve(factor, right_side, left_side=True, lower=True)


def per_device(vectors, diag_blocks, couplings, bounds):
    current_block = vectors[0]
    count_vec, layers, width = current_block.shape
    length_all = lax.axis_size("layer") * layers * width
    bottom = bounds[0, 0].astype(jnp.float32) / 64.0
    summit = bounds[0, 1].astype(jnp.float32) / 64.0
    centre = (bottom + summit) / 2.0
    half_width = (summit - bottom) / 2.0
    arrived_link = shifted(couplings[layers - 1 :], "layer", 1)
    links_below = jnp.concatenate([arrived_link, couplings[: layers - 1]], 0)

    def apply_operator(vectors_now):
        rounded = vectors_now.astype(jnp.bfloat16)
        padded = extended(rounded, (("layer", 1),), 1)
        result = jnp.einsum(
            "kld,lde->kle", rounded, diag_blocks, preferred_element_type=jnp.float32
        )
        result = result + jnp.einsum(
            "kle,lde->kld", padded[:, 2:], couplings, preferred_element_type=jnp.float32
        )
        return result + jnp.einsum(
            "kld,lde->kle", padded[:, :-2], links_below, preferred_element_type=jnp.float32
        )

    def filter_block(start):
        previous = start
        current = (apply_operator(start) - centre * start) / half_width
        for degree_index in range(DEG - 1):
            following = 2.0 * (apply_operator(current) - centre * current) / half_width - previous
            previous = current
            current = following
        return current

    def orthonormal(filtered):
        flat = filtered.reshape(count_vec, layers * width)
        gram = lax.psum(inner_products(flat, flat), "layer") / length_all
        return left_solve(jnp.linalg.cholesky(gram), flat)

    current_block = orthonormal(filter_block(current_block)).reshape(count_vec, layers, width)
    filtered = filter_block(current_block)
    final = orthonormal(filtered)
    low_edge = final[:EDGE]
    high_edge = final[count_vec - EDGE :]
    below_high = shifted(high_edge.astype(jnp.bfloat16), "cuts", 1).astype(high_edge.dtype)
    above_low = shifted(low_edge.astype(jnp.bfloat16), "cuts", -1).astype(low_edge.dtype)
    correlation_low, correlation_high = lax.psum(
        (inner_products(below_high, low_edge), inner_products(above_low, high_edge)), "layer"
    )
    low_new = low_edge - jnp.einsum(
        "wv,wn->vn", correlation_low / length_all, below_high, precision=lax.Precision.HIGHEST
    )
    high_new = high_edge - jnp.einsum(
        "wv,wn->vn", correlation_high / length_all, above_low, precision=lax.Precision.HIGHEST
    )
    result = jnp.concatenate([low_new, final[EDGE : count_vec - EDGE], high_new], 0)
    return result.reshape(1, count_vec, layers, width)


def solution(mesh):
    in_specs = (
        P("cuts", None, "layer", None),
        P("layer", None, None),
        P("layer", None, None),
        P("cuts", None),
    )
    out_specs = P("cuts", None, "layer", None)
    return jax.shard_map(
        per_device, mesh=mesh, in_specs=in_specs, out_specs=out_specs, check_vma=False
    )
```

profile of v0, /device:TPU:138, one launch (start us, length us, event | category | flops | bytes accessed | tf_op | source)
XLA Modules:
  0.0 574.1 jit_solution(272118990598733513)
XLA Ops:
  0.0 2.8 fusion.112
  2.9 2.2 collective-permute-start.1
  5.3 4.3 collective-permute-start.2
  9.6 4.9 collective-permute-start
  14.5 0.9 convolution_bitcast_fusion.8
  17.2 1.4 fusion.24
  18.6 17.0 %collective-permute-done.2 = bf16[64,1,1024]{2,0,1:T(8,128)(2,1)S(1)} collective-permute-done((bf16[64,1,1024]{2,0,1:T(8,128)(2,1)S(1)}, bf16[64,1,1024]{2,0,1:T(8,128)(2,1)S(1)}, u32[]{:S(2)}, u32[]{:S(2)}) %collective-permute-start.2) | collective-permute-done | bytes 131104 | tf_op jit(solution)/shard_map/ppermute | solution.py:21
  35.6 1.0 fusion.123
  36.7 4.5 collective-permute-start.4
  41.1 0.9 fusion.129
  42.0 4.7 collective-permute-start.3
  46.7 0.8 convolution_bitcast_fusion.6
  47.6 1.6 collective-permute-done.3
  49.2 1.6 fusion.124
  50.8 2.5 collective-permute-start.6
  53.3 0.9 fusion.130
  54.2 6.8 %collective-permute-start.5 = (bf16[64,1,1024]{2,0,1:T(8,128)(2,1)S(1)}, bf16[64,1,1024]{2,0,1:T(8,128)(2,1)S(1)}, u32[]{:S(2)}, u32[]{:S(2)}) collective-permute-start(bf16[64,1,1024]{2,0,1:T(8,128)(2,1)S(1)} %get-tuple-element.23), channel_id=1, source_target_pairs={{1,0},{2,1},{3,2},{4,3},{5,4},{6,5},{7,6},{8,7},{9,8},{10,9},{11,1... | collective-permute-start | bytes 393224 | tf_op jit(solution)/shard_map/ppermute | solution.py:24
  61.0 0.8 convolution_bitcast_fusion.5
  61.9 1.6 collective-permute-done.5
  63.5 1.5 fusion.125
  65.0 1.9 collective-permute-start.8
  67.0 0.9 fusion.131
  67.8 7.4 %collective-permute-start.7 = (bf16[64,1,1024]{2,0,1:T(8,128)(2,1)S(1)}, bf16[64,1,1024]{2,0,1:T(8,128)(2,1)S(1)}, u32[]{:S(2)}, u32[]{:S(2)}) collective-permute-start(bf16[64,1,1024]{2,0,1:T(8,128)(2,1)S(1)} %get-tuple-element.21), channel_id=1, source_target_pairs={{1,0},{2,1},{3,2},{4,3},{5,4},{6,5},{7,6},{8,7},{9,8},{10,9},{11,1... | collective-permute-start | bytes 393224 | tf_op jit(solution)/shard_map/ppermute | solution.py:24
  75.2 0.8 convolution_bitcast_fusion.4
  76.1 1.6 collective-permute-done.7
  77.7 1.5 fusion.41
  79.8 134.1 %psum.28 = f32[64,64]{0,1:T(8,128)S(1)} all-reduce(f32[64,64]{0,1:T(8,128)S(1)} %convolution_bitcast_fusion.11), channel_id=1, replica_groups=mesh['cuts'=8,'layer'=32] {'layer'}, use_global_device_ids=true, to_apply=%region_0.0 | all-reduce | flops 4096 | bytes 32768 | tf_op jit(solution)/shard_map/psum | solution.py:72
  214.0 5.8 %cholesky.44 = f32[64,64]{1,0:T(8,128)S(1)} custom-call(f32[64,64]{1,0:T(8,128)S(1)} %fusion.87), custom_call_target="Cholesky" | custom-call | tf_op jit(solution)/shard_map/jit(cholesky)/cholesky | solution.py:73
  219.9 0.7 compare_reduce_fusion.1
  221.2 4.9 custom-call.6
  226.9 1.9 collective-permute-start.10
  228.8 3.0 fusion.132
  231.9 7.5 %collective-permute-start.9 = (bf16[64,1,1024]{2,0,1:T(8,128)(2,1)S(1)}, bf16[64,1,1024]{2,0,1:T(8,128)(2,1)S(1)}, u32[]{:S(2)}, u32[]{:S(2)}) collective-permute-start(bf16[64,1,1024]{2,0,1:T(8,128)(2,1)S(1)} %get-tuple-element.19), channel_id=1, source_target_pairs={{1,0},{2,1},{3,2},{4,3},{5,4},{6,5},{7,6},{8,7},{9,8},{10,9},{11,1... | collective-permute-start | bytes 393224 | tf_op jit(solution)/shard_map/ppermute | solution.py:24
  239.4 0.8 convolution_bitcast_fusion.3
  240.3 1.6 collective-permute-done.9
  241.9 1.4 fusion.126
  243.3 1.9 collective-permute-start.12
  245.3 0.8 fusion.133
  246.1 7.4 %collective-permute-start.11 = (bf16[64,1,1024]{2,0,1:T(8,128)(2,1)S(1)}, bf16[64,1,1024]{2,0,1:T(8,128)(2,1)S(1)}, u32[]{:S(2)}, u32[]{:S(2)}) collective-permute-start(bf16[64,1,1024]{2,0,1:T(8,128)(2,1)S(1)} %get-tuple-element.17), channel_id=1, source_target_pairs={{1,0},{2,1},{3,2},{4,3},{5,4},{6,5},{7,6},{8,7},{9,8},{10,9},{11,1... | collective-permute-start | bytes 393224 | tf_op jit(solution)/shard_map/ppermute | solution.py:24
  253.5 0.8 convolution_bitcast_fusion.2
  254.4 1.6 collective-permute-done.11
  256.0 1.4 fusion.127
  257.5 1.9 collective-permute-start.14
  259.4 0.8 fusion.134
  260.3 7.4 %collective-permute-start.13 = (bf16[64,1,1024]{2,0,1:T(8,128)(2,1)S(1)}, bf16[64,1,1024]{2,0,1:T(8,128)(2,1)S(1)}, u32[]{:S(2)}, u32[]{:S(2)}) collective-permute-start(bf16[64,1,1024]{2,0,1:T(8,128)(2,1)S(1)} %get-tuple-element.15), channel_id=1, source_target_pairs={{1,0},{2,1},{3,2},{4,3},{5,4},{6,5},{7,6},{8,7},{9,8},{10,9},{11,1... | collective-permute-start | bytes 393224 | tf_op jit(solution)/shard_map/ppermute | solution.py:24
  267.7 0.8 convolution_bitcast_fusion.1
  268.5 1.6 collective-permute-done.13
  270.2 1.4 fusion.128
  271.6 1.9 collective-permute-start.16
  273.6 0.8 fusion.135
  274.4 7.6 %collective-permute-start.15 = (bf16[64,1,1024]{2,0,1:T(8,128)(2,1)S(1)}, bf16[64,1,1024]{2,0,1:T(8,128)(2,1)S(1)}, u32[]{:S(2)}, u32[]{:S(2)}) collective-permute-start(bf16[64,1,1024]{2,0,1:T(8,128)(2,1)S(1)} %get-tuple-element.13), channel_id=1, source_target_pairs={{1,0},{2,1},{3,2},{4,3},{5,4},{6,5},{7,6},{8,7},{9,8},{10,9},{11,1... | collective-permute-start | bytes 393224 | tf_op jit(solution)/shard_map/ppermute | solution.py:24
  282.0 0.8 convolution_bitcast_fusion
  282.9 1.4 collective-permute-done.15
  284.3 1.4 fusion.38
  286.3 134.0 %psum.29 = f32[64,64]{0,1:T(8,128)S(1)} all-reduce(f32[64,64]{0,1:T(8,128)S(1)} %convolution_bitcast_fusion.10), channel_id=1, replica_groups=mesh['cuts'=8,'layer'=32] {'layer'}, use_global_device_ids=true, to_apply=%region_3.6 | all-reduce | flops 4096 | bytes 32768 | tf_op jit(solution)/shard_map/psum | solution.py:72
  420.4 5.8 %cholesky.55 = f32[64,64]{1,0:T(8,128)S(1)} custom-call(f32[64,64]{1,0:T(8,128)S(1)} %fusion.84), custom_call_target="Cholesky" | custom-call | tf_op jit(solution)/shard_map/jit(cholesky)/cholesky | solution.py:73
  426.3 0.6 compare_reduce_fusion
  426.9 0.7 fusion.81
  427.6 4.9 custom-call.7
  433.2 3.3 collective-permute-start.17
  436.5 2.6 collective-permute-start.18
  439.6 4.0 collective-permute-done.18
  443.7 128.6 %all-reduce = (f32[16,16]{1,0:T(8,128)S(1)}, f32[16,16]{1,0:T(8,128)S(1)}) all-reduce(f32[16,16]{1,0:T(8,128)S(1)} %fusion.76, f32[16,16]{1,0:T(8,128)S(1)} %fusion.78), channel_id=1, replica_groups=mesh['cuts'=8,'layer'=32] {'layer'}, use_global_device_ids=true, to_apply=%region_5.8 | all-reduce | flops 512 | bytes 4096 | tf_op jit(solution)/shard_map/psum | solution.py:82
  572.9 1.2 reshape.38
  (59 shorter events, 5.6 us)
Async XLA Ops:
  0.0 5.1 copy-start.4
  0.0 14.4 %copy-start = (bf16[2,1024,1024]{2,1,0:T(8,128)(2,1)S(1)}, bf16[2,1024,1024]{2,1,0:T(8,128)(2,1)}, u32[]{:S(2)}) copy-start(bf16[2,1024,1024]{2,1,0:T(8,128)(2,1)} %param.8) | copy-start | bytes 12582916
  2.8 12.5 %copy-start.5 = (s32[1,2]{1,0:T(1,128)S(1)}, s32[1,2]{1,0:T(1,128)}, u32[]{:S(2)}) copy-start(s32[1,2]{1,0:T(1,128)} %param.10) | copy-start | bytes 28
  2.9 14.4 %copy-start.2 = (bf16[2,1024,1024]{2,1,0:T(8,128)(2,1)S(1)}, bf16[2,1024,1024]{2,1,0:T(8,128)(2,1)}, u32[]{:S(2)}) copy-start(bf16[2,1024,1024]{2,1,0:T(8,128)(2,1)} %param.9) | copy-start | bytes 12582916
  2.9 32.7 %collective-permute-start.1 = (bf16[1,1024,1024]{2,1,0:T(8,128)(2,1)S(1)}, bf16[1,1024,1024]{2,1,0:T(8,128)(2,1)S(1)}, u32[]{:S(2)}, u32[]{:S(2)}) collective-permute-start(bf16[1,1024,1024]{2,1,0:T(8,128)(2,1)S(1)} %get-tuple-element.9), channel_id=1, source_target_pairs={{0,1},{1,2},{2,3},{3,4},{4,5},{5,6},{6,7},{7,8},{8,9},{9,10},{10,1... | collective-permute-start | bytes 6291464 | tf_op jit(solution)/shard_map/ppermute | solution.py:13
  5.3 30.3 %collective-permute-start.2 = (bf16[64,1,1024]{2,0,1:T(8,128)(2,1)S(1)}, bf16[64,1,1024]{2,0,1:T(8,128)(2,1)S(1)}, u32[]{:S(2)}, u32[]{:S(2)}) collective-permute-start(bf16[64,1,1024]{2,0,1:T(8,128)(2,1)S(1)} %get-tuple-element.27), channel_id=1, source_target_pairs={{0,1},{1,2},{2,3},{3,4},{4,5},{5,6},{6,7},{7,8},{8,9},{9,10},{10,1... | collective-permute-start | bytes 393224 | tf_op jit(solution)/shard_map/ppermute | solution.py:21
  9.6 7.6 %collective-permute-start = (bf16[64,1,1024]{2,0,1:T(8,128)(2,1)S(1)}, bf16[64,1,1024]{2,0,1:T(8,128)(2,1)S(1)}, u32[]{:S(2)}, u32[]{:S(2)}) collective-permute-start(bf16[64,1,1024]{2,0,1:T(8,128)(2,1)S(1)} %get-tuple-element.28), channel_id=1, source_target_pairs={{1,0},{2,1},{3,2},{4,3},{5,4},{6,5},{7,6},{8,7},{9,8},{10,9},{11,1... | collective-permute-start | bytes 393224 | tf_op jit(solution)/shard_map/ppermute | solution.py:24
  35.6 39.6 %copy-start.6 = (bf16[1,1024,1024]{2,1,0:T(8,128)(2,1)}, bf16[1,1024,1024]{2,1,0:T(8,128)(2,1)S(1)}, u32[]{:S(2)}) copy-start(bf16[1,1024,1024]{2,1,0:T(8,128)(2,1)S(1)} %collective-permute-done.1) | copy-start | bytes 6291460
  36.7 10.1 %collective-permute-start.4 = (bf16[64,1,1024]{2,0,1:T(8,128)(2,1)S(1)}, bf16[64,1,1024]{2,0,1:T(8,128)(2,1)S(1)}, u32[]{:S(2)}, u32[]{:S(2)}) collective-permute-start(bf16[64,1,1024]{2,0,1:T(8,128)(2,1)S(1)} %get-tuple-element.26), channel_id=1, source_target_pairs={{0,1},{1,2},{2,3},{3,4},{4,5},{5,6},{6,7},{7,8},{8,9},{9,10},{10,1... | collective-permute-start | bytes 393224 | tf_op jit(solution)/shard_map/ppermute | solution.py:21
  42.0 7.2 %collective-permute-start.3 = (bf16[64,1,1024]{2,0,1:T(8,128)(2,1)S(1)}, bf16[64,1,1024]{2,0,1:T(8,128)(2,1)S(1)}, u32[]{:S(2)}, u32[]{:S(2)}) collective-permute-start(bf16[64,1,1024]{2,0,1:T(8,128)(2,1)S(1)} %get-tuple-element.25), channel_id=1, source_target_pairs={{1,0},{2,1},{3,2},{4,3},{5,4},{6,5},{7,6},{8,7},{9,8},{10,9},{11,1... | collective-permute-start | bytes 393224 | tf_op jit(solution)/shard_map/ppermute | solution.py:24
  50.8 10.2 %collective-permute-start.6 = (bf16[64,1,1024]{2,0,1:T(8,128)(2,1)S(1)}, bf16[64,1,1024]{2,0,1:T(8,128)(2,1)S(1)}, u32[]{:S(2)}, u32[]{:S(2)}) collective-permute-start(bf16[64,1,1024]{2,0,1:T(8,128)(2,1)S(1)} %get-tuple-element.24), channel_id=1, source_target_pairs={{0,1},{1,2},{2,3},{3,4},{4,5},{5,6},{6,7},{7,8},{8,9},{9,10},{10,1... | collective-permute-start | bytes 393224 | tf_op jit(solution)/shard_map/ppermute | solution.py:21
  54.2 9.3 %collective-permute-start.5 = (bf16[64,1,1024]{2,0,1:T(8,128)(2,1)S(1)}, bf16[64,1,1024]{2,0,1:T(8,128)(2,1)S(1)}, u32[]{:S(2)}, u32[]{:S(2)}) collective-permute-start(bf16[64,1,1024]{2,0,1:T(8,128)(2,1)S(1)} %get-tuple-element.23), channel_id=1, source_target_pairs={{1,0},{2,1},{3,2},{4,3},{5,4},{6,5},{7,6},{8,7},{9,8},{10,9},{11,1... | collective-permute-start | bytes 393224 | tf_op jit(solution)/shard_map/ppermute | solution.py:24
  65.0 10.2 %collective-permute-start.8 = (bf16[64,1,1024]{2,0,1:T(8,128)(2,1)S(1)}, bf16[64,1,1024]{2,0,1:T(8,128)(2,1)S(1)}, u32[]{:S(2)}, u32[]{:S(2)}) collective-permute-start(bf16[64,1,1024]{2,0,1:T(8,128)(2,1)S(1)} %get-tuple-element.22), channel_id=1, source_target_pairs={{0,1},{1,2},{2,3},{3,4},{4,5},{5,6},{6,7},{7,8},{8,9},{9,10},{10,1... | collective-permute-start | bytes 393224 | tf_op jit(solution)/shard_map/ppermute | solution.py:21
  67.8 9.9 %collective-permute-start.7 = (bf16[64,1,1024]{2,0,1:T(8,128)(2,1)S(1)}, bf16[64,1,1024]{2,0,1:T(8,128)(2,1)S(1)}, u32[]{:S(2)}, u32[]{:S(2)}) collective-permute-start(bf16[64,1,1024]{2,0,1:T(8,128)(2,1)S(1)} %get-tuple-element.21), channel_id=1, source_target_pairs={{1,0},{2,1},{3,2},{4,3},{5,4},{6,5},{7,6},{8,7},{9,8},{10,9},{11,1... | collective-permute-start | bytes 393224 | tf_op jit(solution)/shard_map/ppermute | solution.py:24
  226.2 13.2 %copy-start.7 = (bf16[1,1024,1024]{2,1,0:T(8,128)(2,1)S(1)}, bf16[1,1024,1024]{2,1,0:T(8,128)(2,1)}, u32[]{:S(2)}) copy-start(bf16[1,1024,1024]{2,1,0:T(8,128)(2,1)} %copy-done.6) | copy-start | bytes 6291460
  226.9 12.5 %collective-permute-start.10 = (bf16[64,1,1024]{2,0,1:T(8,128)(2,1)S(1)}, bf16[64,1,1024]{2,0,1:T(8,128)(2,1)S(1)}, u32[]{:S(2)}, u32[]{:S(2)}) collective-permute-start(bf16[64,1,1024]{2,0,1:T(8,128)(2,1)S(1)} %get-tuple-element.20), channel_id=1, source_target_pairs={{0,1},{1,2},{2,3},{3,4},{4,5},{5,6},{6,7},{7,8},{8,9},{9,10},{10,1... | collective-permute-start | bytes 393224 | tf_op jit(solution)/shard_map/ppermute | solution.py:21
  231.8 10.0 %copy-start.3 = (bf16[2,1024,1024]{2,1,0:T(8,128)(2,1)S(1)}, bf16[2,1024,1024]{2,1,0:T(8,128)(2,1)}, u32[]{:S(2)}) copy-start(bf16[2,1024,1024]{2,1,0:T(8,128)(2,1)} %param.9) | copy-start | bytes 12582916
  231.9 10.0 %collective-permute-start.9 = (bf16[64,1,1024]{2,0,1:T(8,128)(2,1)S(1)}, bf16[64,1,1024]{2,0,1:T(8,128)(2,1)S(1)}, u32[]{:S(2)}, u32[]{:S(2)}) collective-permute-start(bf16[64,1,1024]{2,0,1:T(8,128)(2,1)S(1)} %get-tuple-element.19), channel_id=1, source_target_pairs={{1,0},{2,1},{3,2},{4,3},{5,4},{6,5},{7,6},{8,7},{9,8},{10,9},{11,1... | collective-permute-start | bytes 393224 | tf_op jit(solution)/shard_map/ppermute | solution.py:24
  240.3 5.0 copy-start.1
  243.3 10.2 %collective-permute-start.12 = (bf16[64,1,1024]{2,0,1:T(8,128)(2,1)S(1)}, bf16[64,1,1024]{2,0,1:T(8,128)(2,1)S(1)}, u32[]{:S(2)}, u32[]{:S(2)}) collective-permute-start(bf16[64,1,1024]{2,0,1:T(8,128)(2,1)S(1)} %get-tuple-element.18), channel_id=1, source_target_pairs={{0,1},{1,2},{2,3},{3,4},{4,5},{5,6},{6,7},{7,8},{8,9},{9,10},{10,1... | collective-permute-start | bytes 393224 | tf_op jit(solution)/shard_map/ppermute | solution.py:21
  246.1 9.9 %collective-permute-start.11 = (bf16[64,1,1024]{2,0,1:T(8,128)(2,1)S(1)}, bf16[64,1,1024]{2,0,1:T(8,128)(2,1)S(1)}, u32[]{:S(2)}, u32[]{:S(2)}) collective-permute-start(bf16[64,1,1024]{2,0,1:T(8,128)(2,1)S(1)} %get-tuple-element.17), channel_id=1, source_target_pairs={{1,0},{2,1},{3,2},{4,3},{5,4},{6,5},{7,6},{8,7},{9,8},{10,9},{11,1... | collective-permute-start | bytes 393224 | tf_op jit(solution)/shard_map/ppermute | solution.py:24
  257.5 10.2 %collective-permute-start.14 = (bf16[64,1,1024]{2,0,1:T(8,128)(2,1)S(1)}, bf16[64,1,1024]{2,0,1:T(8,128)(2,1)S(1)}, u32[]{:S(2)}, u32[]{:S(2)}) collective-permute-start(bf16[64,1,1024]{2,0,1:T(8,128)(2,1)S(1)} %get-tuple-element.16), channel_id=1, source_target_pairs={{0,1},{1,2},{2,3},{3,4},{4,5},{5,6},{6,7},{7,8},{8,9},{9,10},{10,1... | collective-permute-start | bytes 393224 | tf_op jit(solution)/shard_map/ppermute | solution.py:21
  260.3 9.9 %collective-permute-start.13 = (bf16[64,1,1024]{2,0,1:T(8,128)(2,1)S(1)}, bf16[64,1,1024]{2,0,1:T(8,128)(2,1)S(1)}, u32[]{:S(2)}, u32[]{:S(2)}) collective-permute-start(bf16[64,1,1024]{2,0,1:T(8,128)(2,1)S(1)} %get-tuple-element.15), channel_id=1, source_target_pairs={{1,0},{2,1},{3,2},{4,3},{5,4},{6,5},{7,6},{8,7},{9,8},{10,9},{11,1... | collective-permute-start | bytes 393224 | tf_op jit(solution)/shard_map/ppermute | solution.py:24
  271.6 10.4 %collective-permute-start.16 = (bf16[64,1,1024]{2,0,1:T(8,128)(2,1)S(1)}, bf16[64,1,1024]{2,0,1:T(8,128)(2,1)S(1)}, u32[]{:S(2)}, u32[]{:S(2)}) collective-permute-start(bf16[64,1,1024]{2,0,1:T(8,128)(2,1)S(1)} %get-tuple-element.14), channel_id=1, source_target_pairs={{0,1},{1,2},{2,3},{3,4},{4,5},{5,6},{6,7},{7,8},{8,9},{9,10},{10,1... | collective-permute-start | bytes 393224 | tf_op jit(solution)/shard_map/ppermute | solution.py:21
  274.4 9.9 %collective-permute-start.15 = (bf16[64,1,1024]{2,0,1:T(8,128)(2,1)S(1)}, bf16[64,1,1024]{2,0,1:T(8,128)(2,1)S(1)}, u32[]{:S(2)}, u32[]{:S(2)}) collective-permute-start(bf16[64,1,1024]{2,0,1:T(8,128)(2,1)S(1)} %get-tuple-element.13), channel_id=1, source_target_pairs={{1,0},{2,1},{3,2},{4,3},{5,4},{6,5},{7,6},{8,7},{9,8},{10,9},{11,1... | collective-permute-start | bytes 393224 | tf_op jit(solution)/shard_map/ppermute | solution.py:24
  433.2 6.2 %collective-permute-start.17 = (bf16[16,2048]{1,0:T(8,128)(2,1)S(1)}, bf16[16,2048]{1,0:T(8,128)(2,1)S(1)}, u32[]{:S(2)}, u32[]{:S(2)}) collective-permute-start(bf16[16,2048]{1,0:T(8,128)(2,1)S(1)} %get-tuple-element.11), channel_id=1, source_target_pairs={{0,32},{32,64},{64,96},{96,128},{128,160},{160,192},{192,224},{1,3... | collective-permute-start | bytes 196616 | tf_op jit(solution)/shard_map/ppermute | solution.py:13
  436.5 7.1 %collective-permute-start.18 = (bf16[16,2048]{1,0:T(8,128)(2,1)S(1)}, bf16[16,2048]{1,0:T(8,128)(2,1)S(1)}, u32[]{:S(2)}, u32[]{:S(2)}) collective-permute-start(bf16[16,2048]{1,0:T(8,128)(2,1)S(1)} %get-tuple-element.12), channel_id=1, source_target_pairs={{32,0},{64,32},{96,64},{128,96},{160,128},{192,160},{224,192},{33,... | collective-permute-start | bytes 196616 | tf_op jit(solution)/shard_map/ppermute | solution.py:13
where the time goes:
time: 575 us; the launch traced here: 574 us
  blocking collectives  397 us (69%)
  starting transfers between devices  82.6 us (14%)
  waiting for transfers between devices  32.6 us (6%)
  matrix products  30.7 us (5%)
  other arithmetic  24.2 us (4%)
    psum x2, blocking collectives, orthonormal(): gram = lax.psum(inner_products(flat, flat), 'layer') / length_all  268 us
    psum x1, blocking collectives, per_device(): lax.psum((inner_products(below_high, low_edge), inner_products(above_low,...  129 us
    ppermute x8, starting transfers between devices, extended(): lax.ppermute(lax.slice_in_dim(block, 0, width, axis=dim), axis, backward)  53.7 us
    ppermute x8, starting transfers between devices, extended(): lax.ppermute(lax.slice_in_dim(block, block.shape[dim] - width, None, axis...  20.9 us
    ppermute x8, waiting for transfers between devices, extended(): lax.ppermute(lax.slice_in_dim(block, block.shape[dim] - width, None, axis...  17 us
    another operation x6, other arithmetic, orthonormal(): return left_solve(jnp.linalg.cholesky(gram), flat)  13.1 us
    dot_general x8, matrix products, apply_operator(): jnp.einsum('kle,lde->kld', padded[:, 2:], couplings, preferred_element_ty...  11.6 us
  transfers between devices with their start and end apart: 19, of which 10 were waited for; matrix products, arithmetic and copies ran while one was open for 3% of the time, Pallas kernels for 0%

commit v1 on v0

--- a/solution.py
+++ b/solution.py
@@ -69,7 +69,7 @@
 
     def orthonormal(filtered):
         flat = filtered.reshape(count_vec, layers * width)
-        gram = lax.psum(inner_products(flat, flat), "layer") / length_all
+        gram = jnp.sum(lax.all_gather(inner_products(flat, flat), "layer"), axis=0) / length_all
         return left_solve(jnp.linalg.cholesky(gram), flat)
 
     current_block = orthonormal(filter_block(current_block)).reshape(count_vec, layers, width)

time: 575 us -> 389 us (0.68)
  blocking collectives: 397 us -> 210 us
    psum x2 -> x0, blocking collectives: 268 us -> none  [orthonormal(): gram = lax.psum(inner_products(flat, flat), 'layer') / length_all]
    all_gather x0 -> x2, blocking collectives: none -> 80.1 us  [orthonormal(): lax.all_gather(inner_products(flat, flat), 'layer')]
  transfers between devices with their start and end apart: 19 -> 19, of which waited for: 10 -> 10; matrix products, arithmetic and copies ran while one was open for 3% -> 4% of each run, Pallas kernels for 0% -> 0%
where the time goes in v1:
time: 389 us; the launch traced here: 388 us
  blocking collectives  210 us (54%)
  starting transfers between devices  82.7 us (21%)
  waiting for transfers between devices  32.4 us (8%)
  matrix products  30.7 us (8%)
  other arithmetic  24.4 us (6%)
  local copies, waits for them, and re-layouts  5.49 us (1%)
    psum x1, blocking collectives, per_device(): lax.psum((inner_products(below_high, low_edge), inner_products(above_low,...  130 us
    all_gather x2, blocking collectives, orthonormal(): lax.all_gather(inner_products(flat, flat), 'layer')  80.1 us
    ppermute x8, starting transfers between devices, extended(): lax.ppermute(lax.slice_in_dim(block, 0, width, axis=dim), axis, backward)  52 us
    ppermute x8, starting transfers between devices, extended(): lax.ppermute(lax.slice_in_dim(block, block.shape[dim] - width, None, axis...  22.6 us
    ppermute x8, waiting for transfers between devices, extended(): lax.ppermute(lax.slice_in_dim(block, block.shape[dim] - width, None, axis...  16.8 us
    another operation x6, other arithmetic, orthonormal(): return left_solve(jnp.linalg.cholesky(gram), flat)  13.1 us
    dot_general x8, matrix products, apply_operator(): jnp.einsum('kle,lde->kld', padded[:, 2:], couplings, preferred_element_ty...  11.6 us
    ppermute x8, waiting for transfers between devices, extended(): lax.ppermute(lax.slice_in_dim(block, 0, width, axis=dim), axis, backward)  11.2 us
  transfers between devices with their start and end apart: 19, of which 10 were waited for; matrix products, arithmetic and copies ran while one was open for 4% of the time, Pallas kernels for 0%

profile of v1, /device:TPU:138, one launch (start us, length us, event | category | flops | bytes accessed | tf_op | source)
XLA Modules:
  0.0 387.9 jit_solution(13082902717463475343)
XLA Ops:
  0.0 2.8 fusion.112
  2.9 2.3 collective-permute-start.1
  5.4 4.2 %collective-permute-start.2 = (bf16[64,1,1024]{2,0,1:T(8,128)(2,1)S(1)}, bf16[64,1,1024]{2,0,1:T(8,128)(2,1)S(1)}, u32[]{:S(2)}, u32[]{:S(2)}) collective-permute-start(bf16[64,1,1024]{2,0,1:T(8,128)(2,1)S(1)} %get-tuple-element.27), channel_id=1, source_target_pairs={{0,1},{1,2},{2,3},{3,4},{4,5},{5,6},{6,7},{7,8},{8,9},{9,10},{10,1... | collective-permute-start | bytes 393224 | tf_op jit(solution)/shard_map/ppermute | solution.py:21
  9.6 5.0 %collective-permute-start = (bf16[64,1,1024]{2,0,1:T(8,128)(2,1)S(1)}, bf16[64,1,1024]{2,0,1:T(8,128)(2,1)S(1)}, u32[]{:S(2)}, u32[]{:S(2)}) collective-permute-start(bf16[64,1,1024]{2,0,1:T(8,128)(2,1)S(1)} %get-tuple-element.28), channel_id=1, source_target_pairs={{1,0},{2,1},{3,2},{4,3},{5,4},{6,5},{7,6},{8,7},{9,8},{10,9},{11,1... | collective-permute-start | bytes 393224 | tf_op jit(solution)/shard_map/ppermute | solution.py:24
  14.6 0.9 convolution_bitcast_fusion.8
  17.4 1.4 fusion.24
  18.8 16.8 %collective-permute-done.2 = bf16[64,1,1024]{2,0,1:T(8,128)(2,1)S(1)} collective-permute-done((bf16[64,1,1024]{2,0,1:T(8,128)(2,1)S(1)}, bf16[64,1,1024]{2,0,1:T(8,128)(2,1)S(1)}, u32[]{:S(2)}, u32[]{:S(2)}) %collective-permute-start.2) | collective-permute-done | bytes 131104 | tf_op jit(solution)/shard_map/ppermute | solution.py:21
  35.6 1.1 fusion.123
  36.7 4.5 %collective-permute-start.4 = (bf16[64,1,1024]{2,0,1:T(8,128)(2,1)S(1)}, bf16[64,1,1024]{2,0,1:T(8,128)(2,1)S(1)}, u32[]{:S(2)}, u32[]{:S(2)}) collective-permute-start(bf16[64,1,1024]{2,0,1:T(8,128)(2,1)S(1)} %get-tuple-element.26), channel_id=1, source_target_pairs={{0,1},{1,2},{2,3},{3,4},{4,5},{5,6},{6,7},{7,8},{8,9},{9,10},{10,1... | collective-permute-start | bytes 393224 | tf_op jit(solution)/shard_map/ppermute | solution.py:21
  41.2 0.8 fusion.129
  42.0 4.7 %collective-permute-start.3 = (bf16[64,1,1024]{2,0,1:T(8,128)(2,1)S(1)}, bf16[64,1,1024]{2,0,1:T(8,128)(2,1)S(1)}, u32[]{:S(2)}, u32[]{:S(2)}) collective-permute-start(bf16[64,1,1024]{2,0,1:T(8,128)(2,1)S(1)} %get-tuple-element.25), channel_id=1, source_target_pairs={{1,0},{2,1},{3,2},{4,3},{5,4},{6,5},{7,6},{8,7},{9,8},{10,9},{11,1... | collective-permute-start | bytes 393224 | tf_op jit(solution)/shard_map/ppermute | solution.py:24
  46.7 0.8 convolution_bitcast_fusion.6
  47.6 1.6 collective-permute-done.3
  49.2 1.6 fusion.124
  50.8 2.5 collective-permute-start.6
  53.3 0.8 fusion.130
  54.2 6.8 %collective-permute-start.5 = (bf16[64,1,1024]{2,0,1:T(8,128)(2,1)S(1)}, bf16[64,1,1024]{2,0,1:T(8,128)(2,1)S(1)}, u32[]{:S(2)}, u32[]{:S(2)}) collective-permute-start(bf16[64,1,1024]{2,0,1:T(8,128)(2,1)S(1)} %get-tuple-element.23), channel_id=1, source_target_pairs={{1,0},{2,1},{3,2},{4,3},{5,4},{6,5},{7,6},{8,7},{9,8},{10,9},{11,1... | collective-permute-start | bytes 393224 | tf_op jit(solution)/shard_map/ppermute | solution.py:24
  61.0 0.8 convolution_bitcast_fusion.5
  61.9 1.6 collective-permute-done.5
  63.5 1.5 fusion.125
  65.0 1.9 collective-permute-start.8
  66.9 0.8 fusion.131
  67.8 7.4 %collective-permute-start.7 = (bf16[64,1,1024]{2,0,1:T(8,128)(2,1)S(1)}, bf16[64,1,1024]{2,0,1:T(8,128)(2,1)S(1)}, u32[]{:S(2)}, u32[]{:S(2)}) collective-permute-start(bf16[64,1,1024]{2,0,1:T(8,128)(2,1)S(1)} %get-tuple-element.21), channel_id=1, source_target_pairs={{1,0},{2,1},{3,2},{4,3},{5,4},{6,5},{7,6},{8,7},{9,8},{10,9},{11,1... | collective-permute-start | bytes 393224 | tf_op jit(solution)/shard_map/ppermute | solution.py:24
  75.2 0.8 convolution_bitcast_fusion.4
  76.1 1.6 collective-permute-done.7
  77.7 1.5 fusion.41
  79.8 40.2 %all-gather = f32[2048,64]{1,0:T(8,128)S(1)} all-gather(f32[64,64]{1,0:T(8,128)S(1)} %convolution_bitcast_fusion.11), channel_id=2, replica_groups=mesh['cuts'=8,'layer'=32] {'layer'}, dimensions={0}, use_global_device_ids=true | all-gather | bytes 540672 | tf_op jit(solution)/shard_map/all_gather | solution.py:72
  120.2 5.8 %cholesky.44 = f32[64,64]{1,0:T(8,128)S(1)} custom-call(f32[64,64]{1,0:T(8,128)S(1)} %fusion.87), custom_call_target="Cholesky" | custom-call | tf_op jit(solution)/shard_map/jit(cholesky)/cholesky | solution.py:73
  126.1 0.7 compare_reduce_fusion.1
  127.5 4.9 %custom-call.6 = f32[1,64,64]{1,2,0:T(8,128)S(1)} custom-call(f32[1,64,64]{2,1,0:T(8,128)S(1)} %fusion.80), custom_call_target="InvertDiagBlocksLowerTriangular" | custom-call | tf_op jit(solution)/shard_map/triangular_solve/custom-call.0 | solution.py:34
  133.1 2.3 collective-permute-start.10
  135.3 3.0 fusion.132
  138.4 7.2 %collective-permute-start.9 = (bf16[64,1,1024]{2,0,1:T(8,128)(2,1)S(1)}, bf16[64,1,1024]{2,0,1:T(8,128)(2,1)S(1)}, u32[]{:S(2)}, u32[]{:S(2)}) collective-permute-start(bf16[64,1,1024]{2,0,1:T(8,128)(2,1)S(1)} %get-tuple-element.19), channel_id=1, source_target_pairs={{1,0},{2,1},{3,2},{4,3},{5,4},{6,5},{7,6},{8,7},{9,8},{10,9},{11,1... | collective-permute-start | bytes 393224 | tf_op jit(solution)/shard_map/ppermute | solution.py:24
  145.6 0.8 convolution_bitcast_fusion.3
  146.5 1.6 collective-permute-done.9
  148.1 1.4 fusion.126
  149.5 3.5 collective-permute-start.12
  153.0 0.8 fusion.133
  153.9 5.8 %collective-permute-start.11 = (bf16[64,1,1024]{2,0,1:T(8,128)(2,1)S(1)}, bf16[64,1,1024]{2,0,1:T(8,128)(2,1)S(1)}, u32[]{:S(2)}, u32[]{:S(2)}) collective-permute-start(bf16[64,1,1024]{2,0,1:T(8,128)(2,1)S(1)} %get-tuple-element.17), channel_id=1, source_target_pairs={{1,0},{2,1},{3,2},{4,3},{5,4},{6,5},{7,6},{8,7},{9,8},{10,9},{11,1... | collective-permute-start | bytes 393224 | tf_op jit(solution)/shard_map/ppermute | solution.py:24
  159.7 0.8 convolution_bitcast_fusion.2
  160.6 1.6 collective-permute-done.11
  162.2 1.4 fusion.127
  163.7 1.9 collective-permute-start.14
  165.6 0.8 fusion.134
  166.5 7.4 %collective-permute-start.13 = (bf16[64,1,1024]{2,0,1:T(8,128)(2,1)S(1)}, bf16[64,1,1024]{2,0,1:T(8,128)(2,1)S(1)}, u32[]{:S(2)}, u32[]{:S(2)}) collective-permute-start(bf16[64,1,1024]{2,0,1:T(8,128)(2,1)S(1)} %get-tuple-element.15), channel_id=1, source_target_pairs={{1,0},{2,1},{3,2},{4,3},{5,4},{6,5},{7,6},{8,7},{9,8},{10,9},{11,1... | collective-permute-start | bytes 393224 | tf_op jit(solution)/shard_map/ppermute | solution.py:24
  173.9 0.8 convolution_bitcast_fusion.1
  174.7 1.6 collective-permute-done.13
  176.4 1.4 fusion.128
  177.8 1.9 collective-permute-start.16
  179.8 0.8 fusion.135
  180.6 7.6 %collective-permute-start.15 = (bf16[64,1,1024]{2,0,1:T(8,128)(2,1)S(1)}, bf16[64,1,1024]{2,0,1:T(8,128)(2,1)S(1)}, u32[]{:S(2)}, u32[]{:S(2)}) collective-permute-start(bf16[64,1,1024]{2,0,1:T(8,128)(2,1)S(1)} %get-tuple-element.13), channel_id=1, source_target_pairs={{1,0},{2,1},{3,2},{4,3},{5,4},{6,5},{7,6},{8,7},{9,8},{10,9},{11,1... | collective-permute-start | bytes 393224 | tf_op jit(solution)/shard_map/ppermute | solution.py:24
  188.2 0.8 convolution_bitcast_fusion
  189.1 1.4 collective-permute-done.15
  190.5 1.4 fusion.38
  192.6 40.0 %all-gather.1 = f32[2048,64]{1,0:T(8,128)S(1)} all-gather(f32[64,64]{1,0:T(8,128)S(1)} %convolution_bitcast_fusion.10), channel_id=3, replica_groups=mesh['cuts'=8,'layer'=32] {'layer'}, dimensions={0}, use_global_device_ids=true | all-gather | bytes 540672 | tf_op jit(solution)/shard_map/all_gather | solution.py:72
  232.8 5.8 %cholesky.55 = f32[64,64]{1,0:T(8,128)S(1)} custom-call(f32[64,64]{1,0:T(8,128)S(1)} %fusion.84), custom_call_target="Cholesky" | custom-call | tf_op jit(solution)/shard_map/jit(cholesky)/cholesky | solution.py:73
  238.7 0.6 compare_reduce_fusion
  239.3 0.7 fusion.81
  240.0 4.9 %custom-call.7 = f32[1,64,64]{1,2,0:T(8,128)S(1)} custom-call(f32[1,64,64]{2,1,0:T(8,128)S(1)} %fusion.81), custom_call_target="InvertDiagBlocksLowerTriangular" | custom-call | tf_op jit(solution)/shard_map/triangular_solve/custom-call.0 | solution.py:34
  245.6 3.3 collective-permute-start.17
  248.9 2.6 collective-permute-start.18
  252.0 4.0 %collective-permute-done.18 = bf16[16,2048]{1,0:T(8,128)(2,1)S(1)} collective-permute-done((bf16[16,2048]{1,0:T(8,128)(2,1)S(1)}, bf16[16,2048]{1,0:T(8,128)(2,1)S(1)}, u32[]{:S(2)}, u32[]{:S(2)}) %collective-permute-start.18) | collective-permute-done | bytes 65568 | tf_op jit(solution)/shard_map/ppermute | solution.py:13
  256.1 130.0 %all-reduce = (f32[16,16]{1,0:T(8,128)S(1)}, f32[16,16]{1,0:T(8,128)S(1)}) all-reduce(f32[16,16]{1,0:T(8,128)S(1)} %fusion.76, f32[16,16]{1,0:T(8,128)S(1)} %fusion.78), channel_id=1, replica_groups=mesh['cuts'=8,'layer'=32] {'layer'}, use_global_device_ids=true, to_apply=%region_5.8 | all-reduce | flops 512 | bytes 4096 | tf_op jit(solution)/shard_map/psum | solution.py:82
  386.6 1.2 reshape.38
  (67 shorter events, 6.0 us)
Async XLA Ops:
  0.0 5.2 %copy-start.4 = (f32[1,64,2,1024]{3,2,1,0:T(2,128)S(1)}, f32[1,64,2,1024]{3,2,1,0:T(2,128)}, u32[]{:S(2)}) copy-start(f32[1,64,2,1024]{3,2,1,0:T(2,128)} %param.7) | copy-start | bytes 1572868
  0.0 14.6 %copy-start = (bf16[2,1024,1024]{2,1,0:T(8,128)(2,1)S(1)}, bf16[2,1024,1024]{2,1,0:T(8,128)(2,1)}, u32[]{:S(2)}) copy-start(bf16[2,1024,1024]{2,1,0:T(8,128)(2,1)} %param.8) | copy-start | bytes 12582916
  2.8 72.4 %copy-start.5 = (bf16[1,1024,1024]{2,1,0:T(8,128)(2,1)}, bf16[1,1024,1024]{2,1,0:T(8,128)(2,1)S(1)}, u32[]{:S(2)}) copy-start(bf16[1,1024,1024]{2,1,0:T(8,128)(2,1)S(1)} %get-tuple-element.10) | copy-start | bytes 6291460
  2.9 12.6 %copy-start.7 = (s32[1,2]{1,0:T(1,128)S(1)}, s32[1,2]{1,0:T(1,128)}, u32[]{:S(2)}) copy-start(s32[1,2]{1,0:T(1,128)} %param.10) | copy-start | bytes 28
  2.9 14.5 %copy-start.2 = (bf16[2,1024,1024]{2,1,0:T(8,128)(2,1)S(1)}, bf16[2,1024,1024]{2,1,0:T(8,128)(2,1)}, u32[]{:S(2)}) copy-start(bf16[2,1024,1024]{2,1,0:T(8,128)(2,1)} %param.9) | copy-start | bytes 12582916
  2.9 32.7 %collective-permute-start.1 = (bf16[1,1024,1024]{2,1,0:T(8,128)(2,1)S(1)}, bf16[1,1024,1024]{2,1,0:T(8,128)(2,1)S(1)}, u32[]{:S(2)}, u32[]{:S(2)}) collective-permute-start(bf16[1,1024,1024]{2,1,0:T(8,128)(2,1)S(1)} %get-tuple-element.9), channel_id=1, source_target_pairs={{0,1},{1,2},{2,3},{3,4},{4,5},{5,6},{6,7},{7,8},{8,9},{9,10},{10,1... | collective-permute-start | bytes 6291464 | tf_op jit(solution)/shard_map/ppermute | solution.py:13
  5.4 30.2 %collective-permute-start.2 = (bf16[64,1,1024]{2,0,1:T(8,128)(2,1)S(1)}, bf16[64,1,1024]{2,0,1:T(8,128)(2,1)S(1)}, u32[]{:S(2)}, u32[]{:S(2)}) collective-permute-start(bf16[64,1,1024]{2,0,1:T(8,128)(2,1)S(1)} %get-tuple-element.27), channel_id=1, source_target_pairs={{0,1},{1,2},{2,3},{3,4},{4,5},{5,6},{6,7},{7,8},{8,9},{9,10},{10,1... | collective-permute-start | bytes 393224 | tf_op jit(solution)/shard_map/ppermute | solution.py:21
  9.6 7.8 %collective-permute-start = (bf16[64,1,1024]{2,0,1:T(8,128)(2,1)S(1)}, bf16[64,1,1024]{2,0,1:T(8,128)(2,1)S(1)}, u32[]{:S(2)}, u32[]{:S(2)}) collective-permute-start(bf16[64,1,1024]{2,0,1:T(8,128)(2,1)S(1)} %get-tuple-element.28), channel_id=1, source_target_pairs={{1,0},{2,1},{3,2},{4,3},{5,4},{6,5},{7,6},{8,7},{9,8},{10,9},{11,1... | collective-permute-start | bytes 393224 | tf_op jit(solution)/shard_map/ppermute | solution.py:24
  35.6 39.6 %copy-start.8 = (bf16[1,1024,1024]{2,1,0:T(8,128)(2,1)}, bf16[1,1024,1024]{2,1,0:T(8,128)(2,1)S(1)}, u32[]{:S(2)}) copy-start(bf16[1,1024,1024]{2,1,0:T(8,128)(2,1)S(1)} %collective-permute-done.1) | copy-start | bytes 6291460
  36.7 10.0 %collective-permute-start.4 = (bf16[64,1,1024]{2,0,1:T(8,128)(2,1)S(1)}, bf16[64,1,1024]{2,0,1:T(8,128)(2,1)S(1)}, u32[]{:S(2)}, u32[]{:S(2)}) collective-permute-start(bf16[64,1,1024]{2,0,1:T(8,128)(2,1)S(1)} %get-tuple-element.26), channel_id=1, source_target_pairs={{0,1},{1,2},{2,3},{3,4},{4,5},{5,6},{6,7},{7,8},{8,9},{9,10},{10,1... | collective-permute-start | bytes 393224 | tf_op jit(solution)/shard_map/ppermute | solution.py:21
  42.0 7.2 %collective-permute-start.3 = (bf16[64,1,1024]{2,0,1:T(8,128)(2,1)S(1)}, bf16[64,1,1024]{2,0,1:T(8,128)(2,1)S(1)}, u32[]{:S(2)}, u32[]{:S(2)}) collective-permute-start(bf16[64,1,1024]{2,0,1:T(8,128)(2,1)S(1)} %get-tuple-element.25), channel_id=1, source_target_pairs={{1,0},{2,1},{3,2},{4,3},{5,4},{6,5},{7,6},{8,7},{9,8},{10,9},{11,1... | collective-permute-start | bytes 393224 | tf_op jit(solution)/shard_map/ppermute | solution.py:24
  50.8 10.2 %collective-permute-start.6 = (bf16[64,1,1024]{2,0,1:T(8,128)(2,1)S(1)}, bf16[64,1,1024]{2,0,1:T(8,128)(2,1)S(1)}, u32[]{:S(2)}, u32[]{:S(2)}) collective-permute-start(bf16[64,1,1024]{2,0,1:T(8,128)(2,1)S(1)} %get-tuple-element.24), channel_id=1, source_target_pairs={{0,1},{1,2},{2,3},{3,4},{4,5},{5,6},{6,7},{7,8},{8,9},{9,10},{10,1... | collective-permute-start | bytes 393224 | tf_op jit(solution)/shard_map/ppermute | solution.py:21
  54.2 9.3 %collective-permute-start.5 = (bf16[64,1,1024]{2,0,1:T(8,128)(2,1)S(1)}, bf16[64,1,1024]{2,0,1:T(8,128)(2,1)S(1)}, u32[]{:S(2)}, u32[]{:S(2)}) collective-permute-start(bf16[64,1,1024]{2,0,1:T(8,128)(2,1)S(1)} %get-tuple-element.23), channel_id=1, source_target_pairs={{1,0},{2,1},{3,2},{4,3},{5,4},{6,5},{7,6},{8,7},{9,8},{10,9},{11,1... | collective-permute-start | bytes 393224 | tf_op jit(solution)/shard_map/ppermute | solution.py:24
  65.0 10.2 %collective-permute-start.8 = (bf16[64,1,1024]{2,0,1:T(8,128)(2,1)S(1)}, bf16[64,1,1024]{2,0,1:T(8,128)(2,1)S(1)}, u32[]{:S(2)}, u32[]{:S(2)}) collective-permute-start(bf16[64,1,1024]{2,0,1:T(8,128)(2,1)S(1)} %get-tuple-element.22), channel_id=1, source_target_pairs={{0,1},{1,2},{2,3},{3,4},{4,5},{5,6},{6,7},{7,8},{8,9},{9,10},{10,1... | collective-permute-start | bytes 393224 | tf_op jit(solution)/shard_map/ppermute | solution.py:21
  67.8 9.9 %collective-permute-start.7 = (bf16[64,1,1024]{2,0,1:T(8,128)(2,1)S(1)}, bf16[64,1,1024]{2,0,1:T(8,128)(2,1)S(1)}, u32[]{:S(2)}, u32[]{:S(2)}) collective-permute-start(bf16[64,1,1024]{2,0,1:T(8,128)(2,1)S(1)} %get-tuple-element.21), channel_id=1, source_target_pairs={{1,0},{2,1},{3,2},{4,3},{5,4},{6,5},{7,6},{8,7},{9,8},{10,9},{11,1... | collective-permute-start | bytes 393224 | tf_op jit(solution)/shard_map/ppermute | solution.py:24
  120.2 25.4 %copy-start.6 = (bf16[1,1024,1024]{2,1,0:T(8,128)(2,1)S(1)}, bf16[1,1024,1024]{2,1,0:T(8,128)(2,1)}, u32[]{:S(2)}) copy-start(bf16[1,1024,1024]{2,1,0:T(8,128)(2,1)} %copy-done.5) | copy-start | bytes 6291460
  132.4 13.2 %copy-start.9 = (bf16[1,1024,1024]{2,1,0:T(8,128)(2,1)S(1)}, bf16[1,1024,1024]{2,1,0:T(8,128)(2,1)}, u32[]{:S(2)}) copy-start(bf16[1,1024,1024]{2,1,0:T(8,128)(2,1)} %copy-done.8) | copy-start | bytes 6291460
  133.1 12.5 %collective-permute-start.10 = (bf16[64,1,1024]{2,0,1:T(8,128)(2,1)S(1)}, bf16[64,1,1024]{2,0,1:T(8,128)(2,1)S(1)}, u32[]{:S(2)}, u32[]{:S(2)}) collective-permute-start(bf16[64,1,1024]{2,0,1:T(8,128)(2,1)S(1)} %get-tuple-element.20), channel_id=1, source_target_pairs={{0,1},{1,2},{2,3},{3,4},{4,5},{5,6},{6,7},{7,8},{8,9},{9,10},{10,1... | collective-permute-start | bytes 393224 | tf_op jit(solution)/shard_map/ppermute | solution.py:21
  138.4 9.7 %copy-start.3 = (bf16[2,1024,1024]{2,1,0:T(8,128)(2,1)S(1)}, bf16[2,1024,1024]{2,1,0:T(8,128)(2,1)}, u32[]{:S(2)}) copy-start(bf16[2,1024,1024]{2,1,0:T(8,128)(2,1)} %param.9) | copy-start | bytes 12582916
  138.4 9.7 %collective-permute-start.9 = (bf16[64,1,1024]{2,0,1:T(8,128)(2,1)S(1)}, bf16[64,1,1024]{2,0,1:T(8,128)(2,1)S(1)}, u32[]{:S(2)}, u32[]{:S(2)}) collective-permute-start(bf16[64,1,1024]{2,0,1:T(8,128)(2,1)S(1)} %get-tuple-element.19), channel_id=1, source_target_pairs={{1,0},{2,1},{3,2},{4,3},{5,4},{6,5},{7,6},{8,7},{9,8},{10,9},{11,1... | collective-permute-start | bytes 393224 | tf_op jit(solution)/shard_map/ppermute | solution.py:24
  146.5 6.6 %copy-start.1 = (bf16[2,1024,1024]{2,1,0:T(8,128)(2,1)S(1)}, bf16[2,1024,1024]{2,1,0:T(8,128)(2,1)}, u32[]{:S(2)}) copy-start(bf16[2,1024,1024]{2,1,0:T(8,128)(2,1)} %param.8) | copy-start | bytes 12582916
  149.5 10.2 %collective-permute-start.12 = (bf16[64,1,1024]{2,0,1:T(8,128)(2,1)S(1)}, bf16[64,1,1024]{2,0,1:T(8,128)(2,1)S(1)}, u32[]{:S(2)}, u32[]{:S(2)}) collective-permute-start(bf16[64,1,1024]{2,0,1:T(8,128)(2,1)S(1)} %get-tuple-element.18), channel_id=1, source_target_pairs={{0,1},{1,2},{2,3},{3,4},{4,5},{5,6},{6,7},{7,8},{8,9},{9,10},{10,1... | collective-permute-start | bytes 393224 | tf_op jit(solution)/shard_map/ppermute | solution.py:21
  153.9 8.3 %collective-permute-start.11 = (bf16[64,1,1024]{2,0,1:T(8,128)(2,1)S(1)}, bf16[64,1,1024]{2,0,1:T(8,128)(2,1)S(1)}, u32[]{:S(2)}, u32[]{:S(2)}) collective-permute-start(bf16[64,1,1024]{2,0,1:T(8,128)(2,1)S(1)} %get-tuple-element.17), channel_id=1, source_target_pairs={{1,0},{2,1},{3,2},{4,3},{5,4},{6,5},{7,6},{8,7},{9,8},{10,9},{11,1... | collective-permute-start | bytes 393224 | tf_op jit(solution)/shard_map/ppermute | solution.py:24
  163.7 10.2 %collective-permute-start.14 = (bf16[64,1,1024]{2,0,1:T(8,128)(2,1)S(1)}, bf16[64,1,1024]{2,0,1:T(8,128)(2,1)S(1)}, u32[]{:S(2)}, u32[]{:S(2)}) collective-permute-start(bf16[64,1,1024]{2,0,1:T(8,128)(2,1)S(1)} %get-tuple-element.16), channel_id=1, source_target_pairs={{0,1},{1,2},{2,3},{3,4},{4,5},{5,6},{6,7},{7,8},{8,9},{9,10},{10,1... | collective-permute-start | bytes 393224 | tf_op jit(solution)/shard_map/ppermute | solution.py:21
  166.5 9.9 %collective-permute-start.13 = (bf16[64,1,1024]{2,0,1:T(8,128)(2,1)S(1)}, bf16[64,1,1024]{2,0,1:T(8,128)(2,1)S(1)}, u32[]{:S(2)}, u32[]{:S(2)}) collective-permute-start(bf16[64,1,1024]{2,0,1:T(8,128)(2,1)S(1)} %get-tuple-element.15), channel_id=1, source_target_pairs={{1,0},{2,1},{3,2},{4,3},{5,4},{6,5},{7,6},{8,7},{9,8},{10,9},{11,1... | collective-permute-start | bytes 393224 | tf_op jit(solution)/shard_map/ppermute | solution.py:24
  177.8 10.4 %collective-permute-start.16 = (bf16[64,1,1024]{2,0,1:T(8,128)(2,1)S(1)}, bf16[64,1,1024]{2,0,1:T(8,128)(2,1)S(1)}, u32[]{:S(2)}, u32[]{:S(2)}) collective-permute-start(bf16[64,1,1024]{2,0,1:T(8,128)(2,1)S(1)} %get-tuple-element.14), channel_id=1, source_target_pairs={{0,1},{1,2},{2,3},{3,4},{4,5},{5,6},{6,7},{7,8},{8,9},{9,10},{10,1... | collective-permute-start | bytes 393224 | tf_op jit(solution)/shard_map/ppermute | solution.py:21
  180.6 9.9 %collective-permute-start.15 = (bf16[64,1,1024]{2,0,1:T(8,128)(2,1)S(1)}, bf16[64,1,1024]{2,0,1:T(8,128)(2,1)S(1)}, u32[]{:S(2)}, u32[]{:S(2)}) collective-permute-start(bf16[64,1,1024]{2,0,1:T(8,128)(2,1)S(1)} %get-tuple-element.13), channel_id=1, source_target_pairs={{1,0},{2,1},{3,2},{4,3},{5,4},{6,5},{7,6},{8,7},{9,8},{10,9},{11,1... | collective-permute-start | bytes 393224 | tf_op jit(solution)/shard_map/ppermute | solution.py:24
  245.6 6.2 %collective-permute-start.17 = (bf16[16,2048]{1,0:T(8,128)(2,1)S(1)}, bf16[16,2048]{1,0:T(8,128)(2,1)S(1)}, u32[]{:S(2)}, u32[]{:S(2)}) collective-permute-start(bf16[16,2048]{1,0:T(8,128)(2,1)S(1)} %get-tuple-element.11), channel_id=1, source_target_pairs={{0,32},{32,64},{64,96},{96,128},{128,160},{160,192},{192,224},{1,3... | collective-permute-start | bytes 196616 | tf_op jit(solution)/shard_map/ppermute | solution.py:13
  248.9 7.1 %collective-permute-start.18 = (bf16[16,2048]{1,0:T(8,128)(2,1)S(1)}, bf16[16,2048]{1,0:T(8,128)(2,1)S(1)}, u32[]{:S(2)}, u32[]{:S(2)}) collective-permute-start(bf16[16,2048]{1,0:T(8,128)(2,1)S(1)} %get-tuple-element.12), channel_id=1, source_target_pairs={{32,0},{64,32},{96,64},{128,96},{160,128},{192,160},{224,192},{33,... | collective-permute-start | bytes 196616 | tf_op jit(solution)/shard_map/ppermute | solution.py:13
